TPU v7x, 256 devices: a whole 4x4x8 slice. The times are simulated.
256 devices in a mesh: video: 4 (over x), tm: 16 (over z, core), space: 4 (over y).
Axes of the slice: x: 4, y: 4, z: 8, core: 2. Of those that a mesh axis runs over, the one named last changes fastest.
Arguments:
- feature_maps: bfloat16 [64, 128, 240, 128], P(('video', 'tm'), 'space'), parts along dimension 0, may hold values from -27 to 27
- query_frame: int32 [2048], P('video'), parts along dimension 0, may hold values from 0 to 15
- query_row: int32 [2048], P('video'), parts along dimension 0, may hold values from 0 to 127
- query_col: int32 [2048], P('video'), parts along dimension 0, may hold values from 0 to 239
- ema_decay: float32 [64, 128], P(('video', 'tm')), parts along dimension 0, may hold values from 0.14 to 1
- dw_kernel: float32 [3, 128], replicated, may hold values from -3 to 3
- pw_weight: bfloat16 [128, 128], replicated, may hold values from -0.5 to 0.5
- out_weight: float32 [2, 128], replicated, may hold values from -2 to 2
Outputs:
- tracks: float32 [64, 2, 512], P(('video', 'tm')), parts along dimension 0
There are 4 independent parts, one for each index of `video`. A program takes and returns all parts, laid end to end along the dimension named above; an argument that names none is the same for every part. Nothing has to cross between parts.
All inputs are finite; a program needn't handle non-finite values.
Results may differ from a plain program's by a relative error of at most 0.0026.
Values may be sent and summed in bfloat16 or wider, within the bound.
A program may use at most 128 MiB of HBM per device.

v0:
```python
import math
import jax
import jax.numpy as jnp
from jax import lax
from jax.sharding import PartitionSpec as P


def with_halo(cells, sides, width):
    for axis, dim in sides:
        count = lax.axis_size(axis)
        ends = count - 1
        head = lax.slice_in_dim(cells, 0, width, axis=dim)
        tail = lax.slice_in_dim(cells, cells.shape[dim] - width, cells.shape[dim], axis=dim)
        cells = jnp.concatenate(
            [
                lax.ppermute(tail, axis, [(i, (i + 1) % count) for i in range(ends)]),
                cells,
                lax.ppermute(head, axis, [((i + 1) % count, i) for i in range(ends)]),
            ],
            axis=dim,
        )
    return cells


def local(
    feature_maps, query_frame, query_row, query_col, ema_decay, dw_kernel, pw_weight, out_weight
):
    frames_here, rows_here, map_width, channels = feature_maps.shape
    num_queries = query_frame.shape[0]
    first_frame = lax.axis_index("tm") * frames_here
    first_row = lax.axis_index("space") * rows_here
    map_height = rows_here * lax.axis_size("space")
    local_frame = query_frame - first_frame
    local_row = query_row - first_row
    owned = (
        (local_frame >= 0)
        & (local_frame < frames_here)
        & (local_row >= 0)
        & (local_row < rows_here)
    )
    picked = feature_maps[
        jnp.clip(local_frame, 0, frames_here - 1), jnp.clip(local_row, 0, rows_here - 1), query_col
    ]
    contrib = jnp.where(owned[:, None], picked.astype(jnp.float32), 0.0)
    query_feats = lax.psum(contrib, ("tm", "space")).astype(jnp.bfloat16)
    scale = 1.0 / math.sqrt(channels)
    col_coord = jnp.arange(map_width, dtype=jnp.int32).astype(jnp.float32) / map_width
    row_coord = (first_row + jnp.arange(rows_here, dtype=jnp.int32)).astype(
        jnp.float32
    ) / map_height
    highest_list, total_list, pos_list, feat_list = ([], [], [], [])
    frame_index = 0
    frame_map = feature_maps[frame_index].reshape(rows_here * map_width, channels)
    scores = (
        lax.dot_general(
            query_feats, frame_map, (((1,), (1,)), ((), ())), preferred_element_type=jnp.float32
        )
        * scale
    )
    highest = jnp.max(scores, axis=1)
    weights_exp = jnp.exp(scores - highest[:, None])
    highest_list.append(highest)
    total_list.append(jnp.sum(weights_exp, axis=1))
    grid = weights_exp.reshape(num_queries, rows_here, map_width)
    col_part = jnp.sum(jnp.sum(grid, axis=1) * col_coord[None, :], axis=1)
    line_portion = jnp.sum(jnp.sum(grid, axis=2) * row_coord[None, :], axis=1)
    pos_list.append(jnp.stack([col_part, line_portion], 1))
    feat_list.append(
        jnp.dot(weights_exp.astype(jnp.bfloat16), frame_map, preferred_element_type=jnp.float32)
    )
    highest = jnp.stack(highest_list)
    totals = jnp.stack(total_list)
    pos_sum = jnp.stack(pos_list)
    feat_sum = jnp.stack(feat_list)
    top_value = lax.pmax(highest, "space")
    factor = jnp.exp(highest - top_value)
    grand_total, pos_all, feat_all = lax.psum(
        (factor * totals, factor[..., None] * pos_sum, factor[..., None] * feat_sum), "space"
    )
    position = pos_all / grand_total[..., None]
    focused_result = (feat_all / grand_total[..., None]).astype(jnp.bfloat16)
    padded = with_halo(focused_result, (("tm", 0),), 1).astype(jnp.float32)
    depth = jnp.zeros((frames_here, num_queries, channels), jnp.float32)
    for tap in range(dw_kernel.shape[0]):
        depth = depth + dw_kernel[tap][None, None, :] * padded[tap : tap + frames_here]
    hidden = jax.nn.gelu(depth).astype(jnp.bfloat16)
    mixed = jnp.dot(
        hidden.reshape(-1, channels), pw_weight, preferred_element_type=jnp.float32
    ).reshape(frames_here, num_queries, channels)
    refined = focused_result.astype(jnp.float32) + mixed
    carried = jnp.zeros((num_queries, channels), jnp.float32)
    retain_prod = jnp.ones((channels,), jnp.float32)
    local_states, local_prods = ([], [])
    frame_index = 0
    retain = ema_decay[frame_index]
    carried = retain[None, :] * carried + (1.0 - retain[None, :]) * refined[frame_index]
    retain_prod = retain_prod * retain
    local_states.append(carried)
    local_prods.append(retain_prod)
    all_prods, all_ends = (
        lax.all_gather(retain_prod[None], "tm", axis=0, tiled=True),
        lax.all_gather(carried[None], "tm", axis=0, tiled=True),
    )
    position_tm = lax.axis_index("tm")

    def fold_step(source, running):
        advanced = all_prods[source][None, :] * running + all_ends[source]
        return jnp.where(source < position_tm, advanced, running)

    incoming = lax.fori_loop(
        0, lax.axis_size("tm"), fold_step, jnp.zeros((num_queries, channels), jnp.float32)
    )
    memory = jnp.stack(local_states) + jnp.stack(local_prods)[:, None, :] * incoming[None]
    delta = jnp.einsum("tqc,kc->tkq", memory, out_weight, precision=lax.Precision.HIGHEST)
    return jnp.transpose(position, (0, 2, 1)) + delta


def solution(mesh):
    placed = (
        P(("video", "tm"), "space", None, None),
        P("video"),
        P("video"),
        P("video"),
        P(("video", "tm"), None),
        P(),
        P(),
        P(),
    )
    return jax.shard_map(
        local, mesh=mesh, in_specs=placed, out_specs=P(("video", "tm"), None, None), check_vma=False
    )
```

profile of v0, /device:TPU:1, one launch (start us, length us, event | category | flops | bytes accessed | tf_op | source)
XLA Modules:
  0.0 416.0 jit_solution(9454271297745757524)
XLA Ops:
  8.1 3.1 gather_fusion
  11.4 250.4 %all-reduce.5 = bf16[512,128]{1,0:T(8,128)(2,1)S(1)} all-reduce(f32[512,128]{1,0:T(8,128)S(1)} %convert_select_fusion), channel_id=1, replica_groups=mesh['video'=4,'tm'=16,'space'=4] {'tm','space'}, use_global_device_ids=true, to_apply=%region_0.1 | all-reduce | flops 65536 | bytes 393216 | tf_op jit(solution)/shard_map/psum | solution.py:45
  261.8 2.3 multiply_reduce_fusion
  264.1 7.0 %fusion.50 = (f32[512]{0:T(512)S(1)}, f32[512,7680]{1,0:T(8,128)}) fusion(f32[512]{0:T(512)S(1)} %get-tuple-element.139, f32[512,7680]{1,0:T(8,128)S(1)} %get-tuple-element.140), kind=kLoop, calls=%fused_computation.74 | loop fusion | flops 11795968 | bytes 31461376 | tf_op jit(solution)/shard_map/reduce_sum | solution.py:63
  271.1 6.0 %pmax.7 = f32[1,512]{1,0:T(1,128)S(1)} all-reduce(f32[1,512]{1,0:T(1,128)S(1)} %bitcast.66), channel_id=1, replica_groups=mesh['video'=4,'tm'=16,'space'=4] {'space'}, use_global_device_ids=true, to_apply=%region_2.3 | all-reduce | flops 512 | bytes 4096 | tf_op jit(solution)/shard_map/pmax | solution.py:75
  277.1 8.4 %fusion.7 = f32[1,512,128]{2,1,0:T(8,128)} fusion(bf16[7680,128]{1,0:T(8,128)(2,1)S(1)} %bitcast.62, f32[512,7680]{1,0:T(8,128)} %get-tuple-element.135, f32[512]{0:T(512)S(1)} %bitcast.64), kind=kOutput, calls=%fused_computation.11 | convolution fusion | flops 1010630656 | bytes 17958912 | tf_op jit(solution)/shard_map/dot_general | solution.py:69
  285.5 15.7 %copy.10 = f32[512,7680]{0,1:T(8,128)} copy(f32[512,7680]{1,0:T(8,128)} %get-tuple-element.135) | data formatting | bytes 31457280 | tf_op jit(solution)/shard_map/exp | solution.py:61
  301.3 7.9 %fusion.48 = (f32[512,240]{0,1:T(8,128)S(1)}, f32[512,32]{0,1:T(8,128)S(1)}) fusion(f32[512,32,240]{0,2,1:T(8,128)} %bitcast.63), kind=kLoop, calls=%fused_computation.72 | loop fusion | flops 7725056 | bytes 16285696 | tf_op jit(solution)/shard_map/reduce_sum | solution.py:65
  309.4 7.5 %all-reduce = (f32[512]{0:T(512)S(1)}, f32[1,512,2]{1,2,0:T(2,128)S(1)}) all-reduce(f32[512]{0:T(512)S(1)} %bitcast.70, f32[1,512,2]{1,2,0:T(2,128)S(1)} %maximum_multiply_fusion), channel_id=1, replica_groups=mesh['video'=4,'tm'=16,'space'=4] {'space'}, use_global_device_ids=true, to_apply=%region_9.10 | all-reduce | flops 1536 | bytes 12288 | tf_op jit(solution)/shard_map/psum | solution.py:77
  317.0 15.6 %all-reduce.4.cloned.1.call-done = f32[1,512,128]{2,1,0:T(8,128)} async-done(((f32[1,512,128]{2,1,0:T(8,128)}), f32[1,512,128]{2,1,0:T(8,128)}) %all-reduce.4.cloned.1.call-update) | async-done | bytes 262160 | tf_op jit(solution)/shard_map/psum | solution.py:77
  333.7 4.7 %collective-permute-start.1 = (bf16[1,512,128]{2,1,0:T(8,128)(2,1)S(1)}, bf16[1,512,128]{2,1,0:T(8,128)(2,1)S(1)}, u32[]{:S(2)}, u32[]{:S(2)}) collective-permute-start(bf16[1,512,128]{2,1,0:T(8,128)(2,1)S(1)} %divide_convert_fusion), channel_id=1, source_target_pairs={{4,0},{8,4},{12,8},{16,12},{20,16},{24,20},{28,24},{32,28},{36,32}... | collective-permute-start | bytes 393224 | tf_op jit(solution)/shard_map/ppermute | solution.py:18
  338.4 3.1 collective-permute-start
  342.2 1.2 collective-permute-done
  344.5 18.6 %all-gather = f32[16,1,128]{2,1,0:T(1,128)S(1)} all-gather(f32[1,1,128]{2,1,0:T(1,128)S(1)} %bitcast.73), channel_id=1, replica_groups=mesh['video'=4,'tm'=16,'space'=4] {'tm'}, dimensions={0}, use_global_device_ids=true | all-gather | bytes 8704 | tf_op jit(solution)/shard_map/all_gather | solution.py:101
  363.0 26.2 %all-gather.3.cloned.1.call-done = f32[16,512,128]{2,1,0:T(8,128)} async-done(((f32[1,512,128]{2,1,0:T(8,128)}), f32[16,512,128]{2,1,0:T(8,128)}) %all-gather.3.cloned.1.call-update) | async-done | bytes 4194320 | tf_op jit(solution)/shard_map/all_gather | solution.py:102
  389.2 19.0 %while.14 = (s32[]{:T(128)}, f32[512,128]{1,0:T(8,128)S(1)}, s32[]{:T(128)}, f32[16,128]{1,0:T(8,128)S(1)}, f32[16,512,128]{2,1,0:T(8,128)}, /*index=5*/s32[]{:T(128)}, s32[]{:T(128)}) while((s32[]{:T(128)}, f32[512,128]{1,0:T(8,128)S(1)}, s32[]{:T(128)}, f32[16,128]{1,0:T(8,128)S(1)}, f32[16,512,128]{2,1,0:T(8,128)}, ...), condition=%wide.region_12.13_spmd.clone, body=%wide.region_11.12_spmd.clone.sunk | while | flops 262148 | bytes 788081 | solution.py:110
  389.2 1.1 fusion.57
  390.4 1.1 fusion.57
  391.6 1.1 fusion.57
  392.8 1.1 fusion.57
  394.0 1.1 fusion.57
  395.1 1.1 fusion.57
  396.3 1.1 fusion.57
  397.5 1.1 fusion.57
  398.7 1.1 fusion.57
  399.9 1.1 fusion.57
  401.1 1.1 fusion.57
  402.3 1.1 fusion.57
  403.5 1.1 fusion.57
  404.7 1.1 fusion.57
  405.9 1.1 fusion.57
  407.0 1.1 fusion.57
  (48 shorter events, 6.0 us)
Async XLA Ops:
  6.5 1.6 copy-start
  6.5 326.1 %all-reduce.4.cloned.1.call-start = ((), (), s32[]{:S(2)}) async-start(), calls=%async_computation | async-start | bytes 524288 | tf_op jit(solution)/shard_map/psum | solution.py:77
  285.5 103.7 %all-gather.3.cloned.1.call-start = ((), (), s32[]{:S(2)}) async-start(), calls=%async_computation.1 | async-start | bytes 4456448 | tf_op jit(solution)/shard_map/all_gather | solution.py:102
  301.3 8.1 %copy-start.1 = (f32[1,128]{1,0:T(1,128)S(1)}, f32[1,128]{1,0:T(1,128)}, u32[]{:S(2)}) copy-start(f32[1,128]{1,0:T(1,128)} %param.14) | copy-start | bytes 1540
  301.3 15.7 %copy-start.2 = (f32[3,128]{1,0:T(4,128)S(1)}, f32[3,128]{1,0:T(4,128)}, u32[]{:S(2)}) copy-start(f32[3,128]{1,0:T(4,128)} %param.15) | copy-start | bytes 4612
  301.3 42.2 %copy-start.4 = (bf16[128,128]{1,0:T(8,128)(2,1)S(1)}, bf16[128,128]{1,0:T(8,128)(2,1)}, u32[]{:S(2)}) copy-start(bf16[128,128]{1,0:T(8,128)(2,1)} %param.16) | copy-start | bytes 98308
  301.3 106.9 %copy-start.3 = (f32[2,128]{1,0:T(2,128)S(1)}, f32[2,128]{1,0:T(2,128)}, u32[]{:S(2)}) copy-start(f32[2,128]{1,0:T(2,128)} %param.17) | copy-start | bytes 3076
  333.7 8.5 %collective-permute-start.1 = (bf16[1,512,128]{2,1,0:T(8,128)(2,1)S(1)}, bf16[1,512,128]{2,1,0:T(8,128)(2,1)S(1)}, u32[]{:S(2)}, u32[]{:S(2)}) collective-permute-start(bf16[1,512,128]{2,1,0:T(8,128)(2,1)S(1)} %divide_convert_fusion), channel_id=1, source_target_pairs={{4,0},{8,4},{12,8},{16,12},{20,16},{24,20},{28,24},{32,28},{36,32}... | collective-permute-start | bytes 393224 | tf_op jit(solution)/shard_map/ppermute | solution.py:18
  338.4 5.0 %collective-permute-start = (bf16[1,512,128]{2,1,0:T(8,128)(2,1)S(1)}, bf16[1,512,128]{2,1,0:T(8,128)(2,1)S(1)}, u32[]{:S(2)}, u32[]{:S(2)}) collective-permute-start(bf16[1,512,128]{2,1,0:T(8,128)(2,1)S(1)} %divide_convert_fusion), channel_id=1, source_target_pairs={{0,4},{4,8},{8,12},{12,16},{16,20},{20,24},{24,28},{28,32},{32,36}... | collective-permute-start | bytes 393224 | tf_op jit(solution)/shard_map/ppermute | solution.py:16
Sparse Core Ops, SparseCore 0:
  285.6 46.9 all-reduce.3
  344.6 44.5 all-gather.2
where the time goes:
time: 417 us; the launch traced here: 416 us
  blocking collectives  282 us (68%)
  waiting for transfers between devices  43.7 us (10%)
  other arithmetic  36.3 us (9%)
  local copies, waits for them, and re-layouts  19 us (5%)
  between operations  13.6 us (3%)
  matrix products  12.6 us (3%)
  starting transfers between devices  7.84 us (2%)
    psum x1, blocking collectives, local(): query_feats = lax.psum(contrib, ('tm', 'space')).astype(jnp.bfloat16)  250 us
    all_gather x1, waiting for transfers between devices, local(): lax.all_gather(carried[None], 'tm', axis=0, tiled=True)  26.2 us
    all_gather x1, blocking collectives, local(): lax.all_gather(retain_prod[None], 'tm', axis=0, tiled=True)  18.6 us
    select_n x16, other arithmetic, fold_step(): return jnp.where(source < position_tm, advanced, running)  18.4 us
    exp x1, local copies, waits for them, and re-layouts, local(): weights_exp = jnp.exp(scores - highest[:, None])  15.7 us
    psum x1, waiting for transfers between devices, local(): lax.psum((factor * totals, factor[..., None] * pos_sum, factor[..., None]...  15.6 us
    dot_general x1, matrix products, local(): jnp.dot(weights_exp.astype(jnp.bfloat16), frame_map, preferred_element_ty...  8.38 us
  transfers between devices with their start and end apart: 4, of which 4 were waited for; matrix products, arithmetic and copies ran while one was open for 6% of the time, Pallas kernels for 0%

commit v1 on v0

--- a/solution.py
+++ b/solution.py
@@ -42,7 +42,7 @@
         jnp.clip(local_frame, 0, frames_here - 1), jnp.clip(local_row, 0, rows_here - 1), query_col
     ]
     contrib = jnp.where(owned[:, None], picked.astype(jnp.float32), 0.0)
-    query_feats = lax.psum(contrib, ("tm", "space")).astype(jnp.bfloat16)
+    query_feats = jnp.sum(lax.all_gather(contrib, ("tm", "space")), axis=0).astype(jnp.bfloat16)
     scale = 1.0 / math.sqrt(channels)
     col_coord = jnp.arange(map_width, dtype=jnp.int32).astype(jnp.float32) / map_width
     row_coord = (first_row + jnp.arange(rows_here, dtype=jnp.int32)).astype(

time: 417 us -> 290 us (0.70)
  blocking collectives: 282 us -> 32.1 us
  waiting for transfers between devices: 43.7 us -> 158 us
  other arithmetic: 36.3 us -> 44.2 us
    psum x1 -> x0, blocking collectives: 250 us -> none  [local(): query_feats = lax.psum(contrib, ('tm', 'space')).astype(jnp.bfloat16)]
    all_gather x0 -> x1, waiting for transfers between devices: none -> 102 us  [local(): lax.all_gather(contrib, ('tm', 'space'))]
    psum x1, waiting for transfers between devices: 15.6 us -> 28.3 us  [local(): lax.psum((factor * totals, factor[..., None] * pos_sum, factor[..., None]...]
    reduce_sum x0 -> x1, other arithmetic: none -> 6.53 us  [local(): jnp.sum(lax.all_gather(contrib, ('tm', 'space')), axis=0)]
  transfers between devices with their start and end apart: 4 -> 5, of which waited for: 4 -> 5; matrix products, arithmetic and copies ran while one was open for 6% -> 3% of each run, Pallas kernels for 0% -> 0%
where the time goes in v1:
time: 290 us; the launch traced here: 289 us
  waiting for transfers between devices  158 us (54%)
  other arithmetic  44.2 us (15%)
  blocking collectives  32.1 us (11%)
  local copies, waits for them, and re-layouts  19.7 us (7%)
  between operations  13.3 us (5%)
  matrix products  12.6 us (4%)
  starting transfers between devices  7.88 us (3%)
    all_gather x1, waiting for transfers between devices, local(): lax.all_gather(contrib, ('tm', 'space'))  102 us
    psum x1, waiting for transfers between devices, local(): lax.psum((factor * totals, factor[..., None] * pos_sum, factor[..., None]...  28.3 us
    all_gather x1, waiting for transfers between devices, local(): lax.all_gather(carried[None], 'tm', axis=0, tiled=True)  26.2 us
    all_gather x1, blocking collectives, local(): lax.all_gather(retain_prod[None], 'tm', axis=0, tiled=True)  18.6 us
    select_n x16, other arithmetic, fold_step(): return jnp.where(source < position_tm, advanced, running)  18.4 us
    exp x1, local copies, waits for them, and re-layouts, local(): weights_exp = jnp.exp(scores - highest[:, None])  15.6 us
    dot_general x1, matrix products, local(): jnp.dot(weights_exp.astype(jnp.bfloat16), frame_map, preferred_element_ty...  8.38 us
    reduce_sum x2, other arithmetic, local(): col_part = jnp.sum(jnp.sum(grid, axis=1) * col_coord[None, :], axis=1)  7.94 us
  transfers between devices with their start and end apart: 5, of which 5 were waited for; matrix products, arithmetic and copies ran while one was open for 3% of the time, Pallas kernels for 0%

profile of v1, /device:TPU:1, one launch (start us, length us, event | category | flops | bytes accessed | tf_op | source)
XLA Modules:
  0.0 288.7 jit_solution(8108489110198552376)
XLA Ops:
  8.1 3.1 %gather_fusion = bf16[512,128]{1,0:T(8,128)(2,1)S(1)} fusion(bf16[1,32,240,128]{3,2,1,0:T(8,128)(2,1)S(1)} %copy-done, s32[512]{0:T(512)S(1)} %fusion.41), kind=kCustom, calls=%fused_computation | custom fusion | bytes 268288 | tf_op jit(solution)/shard_map/gather | solution.py:41
  13.7 102.1 %all-gather.4.cloned.1.call-done = f32[64,512,128]{2,1,0:T(8,128)} async-done(((f32[1,512,128]{2,1,0:T(8,128)}), f32[64,512,128]{2,1,0:T(8,128)}) %all-gather.4.cloned.1.call-update) | async-done | bytes 16777232 | tf_op jit(solution)/shard_map/all_gather | solution.py:45
  115.7 6.5 %reduce_sum.54 = bf16[512,128]{1,0:T(8,128)(2,1)S(1)} reduce(f32[64,512,128]{2,1,0:T(8,128)} %all-gather.4.cloned.1.call-done, f32[]{:T(128)} %constant.57.clone.1), dimensions={0}, to_apply=%region_0.1 | reduce | flops 4128768 | bytes 16908292 | tf_op jit(solution)/shard_map/reduce_sum | solution.py:45
  122.3 2.3 multiply_reduce_fusion
  124.5 7.0 %fusion.50 = (f32[512]{0:T(512)S(1)}, f32[512,7680]{1,0:T(8,128)}) fusion(f32[512]{0:T(512)S(1)} %get-tuple-element.139, f32[512,7680]{1,0:T(8,128)S(1)} %get-tuple-element.140), kind=kLoop, calls=%fused_computation.74 | loop fusion | flops 11795968 | bytes 31461376 | tf_op jit(solution)/shard_map/reduce_sum | solution.py:63
  131.6 6.5 %pmax.7 = f32[1,512]{1,0:T(1,128)S(1)} all-reduce(f32[1,512]{1,0:T(1,128)S(1)} %bitcast.69), channel_id=1, replica_groups=mesh['video'=4,'tm'=16,'space'=4] {'space'}, use_global_device_ids=true, to_apply=%region_2.3 | all-reduce | flops 512 | bytes 4096 | tf_op jit(solution)/shard_map/pmax | solution.py:75
  138.1 15.6 %copy.10 = f32[512,7680]{0,1:T(8,128)} copy(f32[512,7680]{1,0:T(8,128)} %get-tuple-element.135) | data formatting | bytes 31457280 | tf_op jit(solution)/shard_map/exp | solution.py:61
  153.8 8.4 %fusion.7 = f32[1,512,128]{2,1,0:T(8,128)} fusion(bf16[7680,128]{1,0:T(8,128)(2,1)S(1)} %bitcast.65, f32[512,7680]{1,0:T(8,128)} %get-tuple-element.135, f32[512]{0:T(512)S(1)} %bitcast.67), kind=kOutput, calls=%fused_computation.11 | convolution fusion | flops 1010630656 | bytes 17958912 | tf_op jit(solution)/shard_map/dot_general | solution.py:69
  162.2 7.8 %fusion.48 = (f32[512,240]{0,1:T(8,128)S(1)}, f32[512,32]{0,1:T(8,128)S(1)}) fusion(f32[512,32,240]{0,2,1:T(8,128)} %bitcast.66), kind=kLoop, calls=%fused_computation.72 | loop fusion | flops 7725056 | bytes 16285696 | tf_op jit(solution)/shard_map/reduce_sum | solution.py:65
  170.3 7.0 %all-reduce = (f32[512]{0:T(512)S(1)}, f32[1,512,2]{1,2,0:T(2,128)S(1)}) all-reduce(f32[512]{0:T(512)S(1)} %bitcast.73, f32[1,512,2]{1,2,0:T(2,128)S(1)} %maximum_multiply_fusion), channel_id=1, replica_groups=mesh['video'=4,'tm'=16,'space'=4] {'space'}, use_global_device_ids=true, to_apply=%region_9.10 | all-reduce | flops 1536 | bytes 12288 | tf_op jit(solution)/shard_map/psum | solution.py:77
  177.3 28.3 %all-reduce.3.cloned.1.call-done = f32[1,512,128]{2,1,0:T(8,128)} async-done(((f32[1,512,128]{2,1,0:T(8,128)}), f32[1,512,128]{2,1,0:T(8,128)}) %all-reduce.3.cloned.1.call-update) | async-done | bytes 262160 | tf_op jit(solution)/shard_map/psum | solution.py:77
  206.7 4.7 %collective-permute-start.1 = (bf16[1,512,128]{2,1,0:T(8,128)(2,1)S(1)}, bf16[1,512,128]{2,1,0:T(8,128)(2,1)S(1)}, u32[]{:S(2)}, u32[]{:S(2)}) collective-permute-start(bf16[1,512,128]{2,1,0:T(8,128)(2,1)S(1)} %divide_convert_fusion), channel_id=1, source_target_pairs={{4,0},{8,4},{12,8},{16,12},{20,16},{24,20},{28,24},{32,28},{36,32}... | collective-permute-start | bytes 393224 | tf_op jit(solution)/shard_map/ppermute | solution.py:18
  211.4 3.1 %collective-permute-start = (bf16[1,512,128]{2,1,0:T(8,128)(2,1)S(1)}, bf16[1,512,128]{2,1,0:T(8,128)(2,1)S(1)}, u32[]{:S(2)}, u32[]{:S(2)}) collective-permute-start(bf16[1,512,128]{2,1,0:T(8,128)(2,1)S(1)} %divide_convert_fusion), channel_id=1, source_target_pairs={{0,4},{4,8},{8,12},{12,16},{16,20},{20,24},{24,28},{28,32},{32,36}... | collective-permute-start | bytes 393224 | tf_op jit(solution)/shard_map/ppermute | solution.py:16
  215.2 1.2 collective-permute-done
  217.4 18.6 %all-gather = f32[16,1,128]{2,1,0:T(1,128)S(1)} all-gather(f32[1,1,128]{2,1,0:T(1,128)S(1)} %bitcast.76), channel_id=1, replica_groups=mesh['video'=4,'tm'=16,'space'=4] {'tm'}, dimensions={0}, use_global_device_ids=true | all-gather | bytes 8704 | tf_op jit(solution)/shard_map/all_gather | solution.py:101
  236.0 26.2 %all-gather.6.cloned.1.call-done = f32[16,512,128]{2,1,0:T(8,128)} async-done(((f32[1,512,128]{2,1,0:T(8,128)}), f32[16,512,128]{2,1,0:T(8,128)}) %all-gather.6.cloned.1.call-update) | async-done | bytes 4194320 | tf_op jit(solution)/shard_map/all_gather | solution.py:102
  262.2 19.0 %while.14 = (s32[]{:T(128)}, f32[512,128]{1,0:T(8,128)S(1)}, s32[]{:T(128)}, f32[16,128]{1,0:T(8,128)S(1)}, f32[16,512,128]{2,1,0:T(8,128)}, /*index=5*/s32[]{:T(128)}, s32[]{:T(128)}) while((s32[]{:T(128)}, f32[512,128]{1,0:T(8,128)S(1)}, s32[]{:T(128)}, f32[16,128]{1,0:T(8,128)S(1)}, f32[16,512,128]{2,1,0:T(8,128)}, ...), condition=%wide.region_12.13_spmd.clone, body=%wide.region_11.12_spmd.clone.sunk | while | flops 262148 | bytes 788081 | solution.py:110
  263.4 1.1 fusion.57
  264.5 1.1 fusion.57
  265.7 1.1 fusion.57
  266.9 1.1 fusion.57
  268.1 1.1 fusion.57
  269.3 1.1 fusion.57
  270.5 1.1 fusion.57
  271.7 1.1 fusion.57
  272.9 1.1 fusion.57
  274.1 1.1 fusion.57
  275.3 1.1 fusion.57
  276.4 1.1 fusion.57
  277.6 1.1 fusion.57
  278.8 1.1 fusion.57
  280.0 1.1 fusion.57
  (49 shorter events, 9.3 us)
Async XLA Ops:
  6.5 1.6 copy-start
  6.5 109.2 %all-gather.4.cloned.1.call-start = ((), (), s32[]{:S(2)}) async-start(), calls=%async_computation | async-start | bytes 17039360 | tf_op jit(solution)/shard_map/all_gather | solution.py:45
  12.1 193.4 %all-reduce.3.cloned.1.call-start = ((), (), s32[]{:S(2)}) async-start(), calls=%async_computation.1 | async-start | bytes 524288 | tf_op jit(solution)/shard_map/psum | solution.py:77
  153.7 60.7 %copy-start.1 = (f32[1,128]{1,0:T(1,128)S(1)}, f32[1,128]{1,0:T(1,128)}, u32[]{:S(2)}) copy-start(f32[1,128]{1,0:T(1,128)} %param.14) | copy-start | bytes 1540
  153.8 62.7 %copy-start.3 = (bf16[128,128]{1,0:T(8,128)(2,1)S(1)}, bf16[128,128]{1,0:T(8,128)(2,1)}, u32[]{:S(2)}) copy-start(bf16[128,128]{1,0:T(8,128)(2,1)} %param.16) | copy-start | bytes 98308
  162.1 119.0 %copy-start.2 = (f32[2,128]{1,0:T(2,128)S(1)}, f32[2,128]{1,0:T(2,128)}, u32[]{:S(2)}) copy-start(f32[2,128]{1,0:T(2,128)} %param.17) | copy-start | bytes 3076
  162.2 100.0 %all-gather.6.cloned.1.call-start = ((), (), s32[]{:S(2)}) async-start(), calls=%async_computation.2 | async-start | bytes 4456448 | tf_op jit(solution)/shard_map/all_gather | solution.py:102
  206.7 8.5 %collective-permute-start.1 = (bf16[1,512,128]{2,1,0:T(8,128)(2,1)S(1)}, bf16[1,512,128]{2,1,0:T(8,128)(2,1)S(1)}, u32[]{:S(2)}, u32[]{:S(2)}) collective-permute-start(bf16[1,512,128]{2,1,0:T(8,128)(2,1)S(1)} %divide_convert_fusion), channel_id=1, source_target_pairs={{4,0},{8,4},{12,8},{16,12},{20,16},{24,20},{28,24},{32,28},{36,32}... | collective-permute-start | bytes 393224 | tf_op jit(solution)/shard_map/ppermute | solution.py:18
  211.4 5.0 %collective-permute-start = (bf16[1,512,128]{2,1,0:T(8,128)(2,1)S(1)}, bf16[1,512,128]{2,1,0:T(8,128)(2,1)S(1)}, u32[]{:S(2)}, u32[]{:S(2)}) collective-permute-start(bf16[1,512,128]{2,1,0:T(8,128)(2,1)S(1)} %divide_convert_fusion), channel_id=1, source_target_pairs={{0,4},{4,8},{8,12},{12,16},{16,20},{20,24},{24,28},{28,32},{32,36}... | collective-permute-start | bytes 393224 | tf_op jit(solution)/shard_map/ppermute | solution.py:16
Sparse Core Ops, SparseCore 0:
  12.2 103.4 all-gather.3
  162.3 43.2 all-reduce.2
  217.6 44.5 all-gather.5
